TPU v7x, 512 devices: a whole 4x8x8 slice. The times are simulated.
512 devices in a mesh: rows: 64 (over x, y, core), cols: 8 (over z).
Axes of the slice: x: 4, y: 8, z: 8, core: 2. Of those that a mesh axis runs over, the one named last changes fastest.
Arguments:
- eigvecs: float32 [65536, 2048], P(('rows', 'cols')), may hold values from -6 to 6
- panels: float32 [8, 65536, 256], P('cols', 'rows'), may hold values from -0.375 to 0.375
- tfactors: float32 [2, 256, 256], replicated, may hold values from -0.03125 to 0.03125
- owners: int32 [2], replicated, may hold values from 0 to 7, as said below
Outputs:
- backvecs: float32 [65536, 2048], P('rows', 'cols')
Inputs may be any that keep to these rules, and one draw needn't show every extreme that they name: `owners`: the entries are distinct slots, among them 0 and 7.
All inputs are finite; a program needn't handle non-finite values.
Results may differ from a plain program's by a relative error of at most 0.00011.
Values sent between devices are 32-bit elements; how exact they have to be, the bound alone decides.
No kernel may reach another device: no remote copies, remote signals or barrier semaphores. Data moves between devices by JAX's collectives and lax.ppermute only.
A program may use at most 64 MiB of HBM per device.

v0:
```python
import jax
import jax.numpy as jnp
from jax import lax
from jax.sharding import Mesh, PartitionSpec as P

PLANE = ("x", "y")


def dot(left, right, dims):
    return lax.dot_general(
        left,
        right,
        (dims, ((), ())),
        precision=lax.Precision.HIGH,
        preferred_element_type=jnp.float32,
    )


def tn(left, right):
    return dot(left, right, ((0,), (0,)))


def nn(left, right):
    return dot(left, right, ((1,), (0,)))


def shift(value, by):
    count = lax.axis_size("z")
    return lax.ppermute(value, "z", [(slot, (slot + by) % count) for slot in range(count)])


def owner_quarters(local):
    quarter = local.shape[0] // 4
    last = lax.axis_index("z") == lax.axis_size("z") - 1
    starts = [jnp.where(last, (3 - step) * quarter, step * quarter) for step in range(4)]
    return [lax.dynamic_slice_in_dim(local, start, quarter) for start in starts]


def scatter_quarters(pieces):
    slot = lax.axis_index("z")
    last = lax.axis_size("z") - 1
    chunk = pieces[0]
    for step in range(1, 4):
        piece = lax.ppermute(pieces[step], "z", [(0, step), (last, last - step)])
        chunk = jnp.where((slot == step) | (slot == last - step), piece, chunk)
    return chunk


def gather_panels(chunk):
    rows, width = chunk.shape
    before2, after2 = (shift(chunk, 2), shift(chunk, -2))
    before1, after1 = (shift(chunk, 1), shift(chunk, -1))
    after3, before3 = (shift(after2, -1), shift(before2, 1))
    across = jnp.concatenate([shift(after2[: rows // 2], -2), shift(before2[rows // 2 :], 2)])
    before, after = ([chunk, before1, before2, before3], [chunk, after1, after2, after3])
    slot = lax.axis_index("z")
    both = jnp.zeros((8, rows, width), chunk.dtype)
    for by, piece in enumerate(before):
        both = lax.dynamic_update_index_in_dim(both, piece, (slot - by) % 8, 0)
    for by, piece in enumerate(after[1:]):
        both = lax.dynamic_update_index_in_dim(both, piece, (slot + by + 1) % 8, 0)
    both = lax.dynamic_update_index_in_dim(both, across, (slot + 4) % 8, 0)
    return both.reshape(2, 4 * rows, width)


def products(first, second, tiles, half):
    width = tiles.shape[1] // 2
    tiles, other = (
        lax.dynamic_slice_in_dim(value, half * width, width, 1) for value in (tiles, first)
    )
    return jnp.concatenate([tn(first, tiles), tn(second, tiles), tn(second, other)])


def reduce_rows(first, second, tiles):
    core = lax.axis_index("c")
    other = products(first, second, tiles, 1 - core)
    other = lax.ppermute(other, "c", [(0, 1), (1, 0)])
    part = products(first, second, tiles, core) + other
    rows, columns = part.shape
    planes = lax.axis_size("x") * lax.axis_size("y")
    pieces = part.reshape(planes, rows // planes, columns)
    pieces = lax.all_to_all(pieces, PLANE, split_axis=0, concat_axis=0, tiled=True)
    pieces = jnp.broadcast_to(pieces.sum(0)[None], pieces.shape)
    pieces = lax.all_to_all(pieces, PLANE, split_axis=0, concat_axis=0, tiled=True)
    return lax.all_gather(pieces.reshape(rows, columns), "c", axis=1, tiled=True)


def per_device(eigvecs, panels, tfactors, owners):
    pieces = owner_quarters(panels[0])
    pieces, eigvecs = lax.optimization_barrier((pieces, eigvecs))
    chunk = scatter_quarters(pieces)
    factors = jnp.triu(tfactors)
    count = lax.axis_size("z")
    tiles = eigvecs.reshape(eigvecs.shape[0], count, -1).swapaxes(0, 1)
    chunk, tiles, factors = lax.optimization_barrier((chunk, tiles, factors))
    tiles = lax.all_to_all(tiles, "z", split_axis=0, concat_axis=0, tiled=True)
    tiles = tiles.reshape(-1, tiles.shape[2])
    both = gather_panels(chunk)
    lead = jnp.where(owners[0] == 0, 0, 1)
    first = lax.dynamic_index_in_dim(both, lead, 0, False)
    second = lax.dynamic_index_in_dim(both, 1 - lead, 0, False)
    width = first.shape[1]
    total = reduce_rows(first, second, tiles)
    proj_first, proj_second, cross = (total[:width], total[width : 2 * width], total[2 * width :])
    coeff_first = nn(factors[0], proj_first)
    coeff_second = nn(factors[1], proj_second - nn(cross, coeff_first))
    return tiles - nn(first, coeff_first) - nn(second, coeff_second)


def solution(mesh):
    split = Mesh(mesh.devices.reshape(4, 8, 2, 8), ("x", "y", "c", "z"))
    rows = ("x", "y", "c")
    placed = (P(rows + ("z",), None), P("z", rows, None), P(), P())
    return jax.shard_map(
        per_device, mesh=split, in_specs=placed, out_specs=P(rows, "z"), check_vma=False
    )
```

profile of v0, /device:TPU:1, one launch (start us, length us, event | category | flops | bytes accessed | tf_op | source)
XLA Modules:
  0.0 146.7 jit_solution(18208789601227877676)
XLA Ops:
  0.0 0.0 copy-start.1
  0.0 0.0 copy-start.2
  0.0 1.4 dynamic-slice_bitcast_fusion
  1.4 8.5 %collective-permute-start = (f32[256,256]{1,0:T(8,128)S(1)}, f32[256,256]{1,0:T(8,128)S(1)}, u32[]{:S(2)}, u32[]{:S(2)}) collective-permute-start(f32[256,256]{1,0:T(8,128)S(1)} %get-tuple-element.13), channel_id=1, source_target_pairs={{0,3},{7,4},{8,11},{15,12},{16,19},{23,20},{24,27},{31,28},{32,35}... | collective-permute-start | bytes 786440 | tf_op jit(solution)/shard_map/ppermute | solution.py:44
  9.9 2.0 %collective-permute-start.1 = (f32[256,256]{1,0:T(8,128)S(1)}, f32[256,256]{1,0:T(8,128)}, u32[]{:S(2)}, u32[]{:S(2)}) collective-permute-start(f32[256,256]{1,0:T(8,128)S(1)} %get-tuple-element.14), channel_id=1, source_target_pairs={{0,2},{7,5},{8,10},{15,13},{16,18},{23,21},{24,26},{31,29},{32,34}... | collective-permute-start | bytes 786440 | tf_op jit(solution)/shard_map/ppermute | solution.py:44
  11.9 2.0 %collective-permute-start.2 = (f32[256,256]{1,0:T(8,128)S(1)}, f32[256,256]{1,0:T(8,128)}, u32[]{:S(2)}, u32[]{:S(2)}) collective-permute-start(f32[256,256]{1,0:T(8,128)S(1)} %get-tuple-element.15), channel_id=1, source_target_pairs={{0,1},{7,6},{8,9},{15,14},{16,17},{23,22},{24,25},{31,30},{32,33},... | collective-permute-start | bytes 786440 | tf_op jit(solution)/shard_map/ppermute | solution.py:44
  13.9 0.1 iota_compare_fusion
  14.0 0.0 copy-done.1
  14.0 0.0 copy-start.3
  14.0 1.1 copy.8
  15.1 0.0 copy-done.2
  15.1 0.8 broadcast_select_fusion
  15.9 0.0 collective-permute-done
  15.9 4.5 %collective-permute-done.1 = f32[256,256]{1,0:T(8,128)} collective-permute-done((f32[256,256]{1,0:T(8,128)S(1)}, f32[256,256]{1,0:T(8,128)}, u32[]{:S(2)}, u32[]{:S(2)}) %collective-permute-start.1) | collective-permute-done | bytes 262176 | tf_op jit(solution)/shard_map/ppermute | solution.py:44
  20.4 5.6 %collective-permute-done.2 = f32[256,256]{1,0:T(8,128)} collective-permute-done((f32[256,256]{1,0:T(8,128)S(1)}, f32[256,256]{1,0:T(8,128)}, u32[]{:S(2)}, u32[]{:S(2)}) %collective-permute-start.2) | collective-permute-done | bytes 262176 | tf_op jit(solution)/shard_map/ppermute | solution.py:44
  26.0 0.1 select_select_fusion
  26.1 1.9 %collective-permute-start.4 = (f32[256,256]{1,0:T(8,128)S(1)}, f32[256,256]{1,0:T(8,128)}, u32[]{:S(2)}, u32[]{:S(2)}) collective-permute-start(f32[256,256]{1,0:T(8,128)S(1)} %select_select_fusion), channel_id=1, source_target_pairs={{0,2},{1,3},{2,4},{3,5},{4,6},{5,7},{6,0},{7,1},{8,10},{9,11},{10,... | collective-permute-start | bytes 786440 | tf_op jit(solution)/shard_map/ppermute | solution.py:29
  28.0 8.2 %collective-permute-start.7 = (f32[256,256]{1,0:T(8,128)S(1)}, f32[256,256]{1,0:T(8,128)}, u32[]{:S(2)}, u32[]{:S(2)}) collective-permute-start(f32[256,256]{1,0:T(8,128)S(1)} %select_select_fusion), channel_id=1, source_target_pairs={{0,6},{1,7},{2,0},{3,1},{4,2},{5,3},{6,4},{7,5},{8,14},{9,15},{10,... | collective-permute-start | bytes 786440 | tf_op jit(solution)/shard_map/ppermute | solution.py:29
  36.2 2.5 %collective-permute-start.3 = (f32[256,256]{1,0:T(8,128)S(1)}, f32[256,256]{1,0:T(8,128)}, u32[]{:S(2)}, u32[]{:S(2)}) collective-permute-start(f32[256,256]{1,0:T(8,128)S(1)} %select_select_fusion), channel_id=1, source_target_pairs={{0,1},{1,2},{2,3},{3,4},{4,5},{5,6},{6,7},{7,0},{8,9},{9,10},{10,1... | collective-permute-start | bytes 786440 | tf_op jit(solution)/shard_map/ppermute | solution.py:29
  38.8 0.0 copy-done.3
  38.9 4.0 %collective-permute-start.6 = (f32[256,256]{1,0:T(8,128)S(1)}, f32[256,256]{1,0:T(8,128)}, u32[]{:S(2)}, u32[]{:S(2)}) collective-permute-start(f32[256,256]{1,0:T(8,128)S(1)} %select_select_fusion), channel_id=1, source_target_pairs={{0,7},{1,0},{2,1},{3,2},{4,3},{5,4},{6,5},{7,6},{8,15},{9,8},{10,9... | collective-permute-start | bytes 786440 | tf_op jit(solution)/shard_map/ppermute | solution.py:29
  42.9 3.6 %all-to-all-start = ((f32[8,128,256]{2,1,0:T(8,128)}), f32[8,128,256]{2,1,0:T(8,128)S(1)}, u32[]{:S(2)}, u32[]{:S(2)}) async-start(f32[8,128,256]{2,1,0:T(8,128)} %bitcast.71), calls=%async_computation | async-start | bytes 2097152 | tf_op jit(solution)/shard_map/all_to_all | solution.py:96
  46.5 0.2 broadcast_in_dim.44
  46.7 0.0 collective-permute-done.4
  46.7 0.9 slice.33
  47.6 4.2 %collective-permute-start.10 = (f32[128,256]{1,0:T(8,128)S(1)}, f32[128,256]{1,0:T(8,128)S(1)}, u32[]{:S(2)}, u32[]{:S(2)}) collective-permute-start(f32[128,256]{1,0:T(8,128)S(1)} %slice.33), channel_id=1, source_target_pairs={{0,2},{1,3},{2,4},{3,5},{4,6},{5,7},{6,0},{7,1},{8,10},{9,11},{10,... | collective-permute-start | bytes 393224 | tf_op jit(solution)/shard_map/ppermute | solution.py:29
  51.8 0.0 collective-permute-done.7
  51.8 0.9 slice.32
  52.8 3.2 %collective-permute-start.9 = (f32[128,256]{1,0:T(8,128)S(1)}, f32[128,256]{1,0:T(8,128)S(1)}, u32[]{:S(2)}, u32[]{:S(2)}) collective-permute-start(f32[128,256]{1,0:T(8,128)S(1)} %slice.32), channel_id=1, source_target_pairs={{0,6},{1,7},{2,0},{3,1},{4,2},{5,3},{6,4},{7,5},{8,14},{9,15},{10,... | collective-permute-start | bytes 393224 | tf_op jit(solution)/shard_map/ppermute | solution.py:29
  56.0 3.3 %collective-permute-start.5 = (f32[256,256]{1,0:T(8,128)}, f32[256,256]{1,0:T(8,128)S(1)}, u32[]{:S(2)}, u32[]{:S(2)}) collective-permute-start(f32[256,256]{1,0:T(8,128)} %collective-permute-done.4), channel_id=1, source_target_pairs={{0,1},{1,2},{2,3},{3,4},{4,5},{5,6},{6,7},{7,0},{8,9},{9,10},{10,1... | collective-permute-start | bytes 786440 | tf_op jit(solution)/shard_map/ppermute | solution.py:29
  59.3 0.0 collective-permute-done.3
  59.3 3.2 %collective-permute-start.8 = (f32[256,256]{1,0:T(8,128)}, f32[256,256]{1,0:T(8,128)S(1)}, u32[]{:S(2)}, u32[]{:S(2)}) collective-permute-start(f32[256,256]{1,0:T(8,128)} %collective-permute-done.7), channel_id=1, source_target_pairs={{0,7},{1,0},{2,1},{3,2},{4,3},{5,4},{6,5},{7,6},{8,15},{9,8},{10,9... | collective-permute-start | bytes 786440 | tf_op jit(solution)/shard_map/ppermute | solution.py:29
  62.5 1.0 bitcast_dynamic-update-slice_fusion.5
  63.5 1.0 bitcast_dynamic-update-slice_fusion.4
  64.5 20.9 %collective-permute-done.5 = f32[256,256]{1,0:T(8,128)S(1)} collective-permute-done((f32[256,256]{1,0:T(8,128)}, f32[256,256]{1,0:T(8,128)S(1)}, u32[]{:S(2)}, u32[]{:S(2)}) %collective-permute-start.5) | collective-permute-done | bytes 262176 | tf_op jit(solution)/shard_map/ppermute | solution.py:29
  85.4 0.0 collective-permute-done.6
  85.4 1.0 bitcast_dynamic-update-slice_fusion.2
  86.4 1.0 bitcast_dynamic-update-slice_fusion.1
  87.3 0.0 collective-permute-done.8
  87.4 0.0 collective-permute-done.10
  87.4 0.0 collective-permute-done.9
  87.4 1.2 fusion.1
  88.6 0.0 all-to-all-done
  88.6 1.0 fusion.10
  89.6 1.0 fusion.3
  90.6 0.8 pad_maximum_fusion
  91.4 2.4 %collective-permute-start.11 = (f32[768,128]{1,0:T(8,128)}, f32[768,128]{1,0:T(8,128)S(1)}, u32[]{:S(2)}, u32[]{:S(2)}) collective-permute-start(f32[768,128]{1,0:T(8,128)} %pad_maximum_fusion), channel_id=1, source_target_pairs={{0,8},{8,0},{1,9},{9,1},{2,10},{10,2},{3,11},{11,3},{4,12},{12,4},... | collective-permute-start | bytes 1179656 | tf_op jit(solution)/shard_map/ppermute | solution.py:77
  93.8 1.2 fusion.5
  95.0 1.0 fusion.12
  96.0 1.0 fusion.7
  97.0 0.0 collective-permute-done.11
  97.1 21.7 %all_to_all.15 = f32[32,24,128]{2,1,0:T(8,128)S(1)} all-to-all(f32[32,24,128]{2,1,0:T(8,128)S(1)} %bitcast.86), channel_id=1, replica_groups=mesh['x'=4,'y'=8,'c'=2,'z'=8] {'x','y'}, dimensions={0} | all-to-all | bytes 786432 | tf_op jit(solution)/shard_map/all_to_all | solution.py:82
  118.8 0.0 copy-start
  118.9 18.6 %all_to_all.16 = f32[32,24,128]{2,1,0:T(8,128)S(1)} all-to-all(f32[32,24,128]{2,1,0:T(8,128)S(1)} %broadcast_in_dim.53), channel_id=1, replica_groups=mesh['x'=4,'y'=8,'c'=2,'z'=8] {'x','y'}, dimensions={0} | all-to-all | bytes 786432 | tf_op jit(solution)/shard_map/all_to_all | solution.py:84
  137.5 6.2 %all_gather.3 = f32[768,256]{1,0:T(8,128)S(1)} all-gather(f32[768,128]{1,0:T(8,128)S(1)} %bitcast.87), channel_id=1, replica_groups=mesh['x'=4,'y'=8,'c'=2,'z'=8] {'c'}, dimensions={1}, use_global_device_ids=true | all-gather | bytes 1179648 | tf_op jit(solution)/shard_map/all_gather | solution.py:85
  143.7 0.0 copy-done
  143.7 0.3 fusion.31
  144.0 0.3 convolution_subtract_fusion.2
  144.2 0.6 convolution_subtract_fusion.1
  144.8 0.3 fusion.34
  145.1 1.6 %convolution_subtract_fusion = f32[1024,256]{1,0:T(8,128)} fusion(f32[1024,256]{1,0:T(8,128)S(1)} %convolution_subtract_fusion.1, f32[256,256]{1,0:T(8,128)S(1)} %fusion.34, f32[2,1024,256]{2,1,0:T(8,128)S(1)} %bitcast.80, s32[]{:T(128)S(6)} %select_n.156), kind=kOutput, calls=%fused_computation | convolution fusion | flops 402915328 | bytes 3407876 | tf_op jit(solution)/shard_map/dot_general | solution.py:10
  (8 shorter events, 0.2 us)
Async XLA Ops:
  0.0 14.0 %copy-start.1 = (f32[128,2048]{1,0:T(8,128)S(1)}, f32[128,2048]{1,0:T(8,128)}, u32[]{:S(2)}) copy-start(f32[128,2048]{1,0:T(8,128)} %param.4) | copy-start | bytes 3145732
  0.0 15.1 %copy-start.2 = (f32[2,256,256]{2,1,0:T(8,128)S(1)}, f32[2,256,256]{2,1,0:T(8,128)}, u32[]{:S(2)}) copy-start(f32[2,256,256]{2,1,0:T(8,128)} %param.6) | copy-start | bytes 1572868
  1.4 14.5 %collective-permute-start = (f32[256,256]{1,0:T(8,128)S(1)}, f32[256,256]{1,0:T(8,128)S(1)}, u32[]{:S(2)}, u32[]{:S(2)}) collective-permute-start(f32[256,256]{1,0:T(8,128)S(1)} %get-tuple-element.13), channel_id=1, source_target_pairs={{0,3},{7,4},{8,11},{15,12},{16,19},{23,20},{24,27},{31,28},{32,35}... | collective-permute-start | bytes 786440 | tf_op jit(solution)/shard_map/ppermute | solution.py:44
  9.9 10.6 %collective-permute-start.1 = (f32[256,256]{1,0:T(8,128)S(1)}, f32[256,256]{1,0:T(8,128)}, u32[]{:S(2)}, u32[]{:S(2)}) collective-permute-start(f32[256,256]{1,0:T(8,128)S(1)} %get-tuple-element.14), channel_id=1, source_target_pairs={{0,2},{7,5},{8,10},{15,13},{16,18},{23,21},{24,26},{31,29},{32,34}... | collective-permute-start | bytes 786440 | tf_op jit(solution)/shard_map/ppermute | solution.py:44
  11.9 14.2 %collective-permute-start.2 = (f32[256,256]{1,0:T(8,128)S(1)}, f32[256,256]{1,0:T(8,128)}, u32[]{:S(2)}, u32[]{:S(2)}) collective-permute-start(f32[256,256]{1,0:T(8,128)S(1)} %get-tuple-element.15), channel_id=1, source_target_pairs={{0,1},{7,6},{8,9},{15,14},{16,17},{23,22},{24,25},{31,30},{32,33},... | collective-permute-start | bytes 786440 | tf_op jit(solution)/shard_map/ppermute | solution.py:44
  14.0 24.8 %copy-start.3 = (s32[2]{0:T(128)S(1)}, s32[2]{0:T(128)}, u32[]{:S(2)}) copy-start(s32[2]{0:T(128)} %param.7) | copy-start | bytes 28
  26.1 20.6 %collective-permute-start.4 = (f32[256,256]{1,0:T(8,128)S(1)}, f32[256,256]{1,0:T(8,128)}, u32[]{:S(2)}, u32[]{:S(2)}) collective-permute-start(f32[256,256]{1,0:T(8,128)S(1)} %select_select_fusion), channel_id=1, source_target_pairs={{0,2},{1,3},{2,4},{3,5},{4,6},{5,7},{6,0},{7,1},{8,10},{9,11},{10,... | collective-permute-start | bytes 786440 | tf_op jit(solution)/shard_map/ppermute | solution.py:29
  28.0 23.8 %collective-permute-start.7 = (f32[256,256]{1,0:T(8,128)S(1)}, f32[256,256]{1,0:T(8,128)}, u32[]{:S(2)}, u32[]{:S(2)}) collective-permute-start(f32[256,256]{1,0:T(8,128)S(1)} %select_select_fusion), channel_id=1, source_target_pairs={{0,6},{1,7},{2,0},{3,1},{4,2},{5,3},{6,4},{7,5},{8,14},{9,15},{10,... | collective-permute-start | bytes 786440 | tf_op jit(solution)/shard_map/ppermute | solution.py:29
  36.2 23.0 %collective-permute-start.3 = (f32[256,256]{1,0:T(8,128)S(1)}, f32[256,256]{1,0:T(8,128)}, u32[]{:S(2)}, u32[]{:S(2)}) collective-permute-start(f32[256,256]{1,0:T(8,128)S(1)} %select_select_fusion), channel_id=1, source_target_pairs={{0,1},{1,2},{2,3},{3,4},{4,5},{5,6},{6,7},{7,0},{8,9},{9,10},{10,1... | collective-permute-start | bytes 786440 | tf_op jit(solution)/shard_map/ppermute | solution.py:29
  38.9 46.5 %collective-permute-start.6 = (f32[256,256]{1,0:T(8,128)S(1)}, f32[256,256]{1,0:T(8,128)}, u32[]{:S(2)}, u32[]{:S(2)}) collective-permute-start(f32[256,256]{1,0:T(8,128)S(1)} %select_select_fusion), channel_id=1, source_target_pairs={{0,7},{1,0},{2,1},{3,2},{4,3},{5,4},{6,5},{7,6},{8,15},{9,8},{10,9... | collective-permute-start | bytes 786440 | tf_op jit(solution)/shard_map/ppermute | solution.py:29
  42.9 45.7 %all-to-all-start = ((f32[8,128,256]{2,1,0:T(8,128)}), f32[8,128,256]{2,1,0:T(8,128)S(1)}, u32[]{:S(2)}, u32[]{:S(2)}) async-start(f32[8,128,256]{2,1,0:T(8,128)} %bitcast.71), calls=%async_computation | async-start | bytes 2097152 | tf_op jit(solution)/shard_map/all_to_all | solution.py:96
  47.6 39.7 %collective-permute-start.10 = (f32[128,256]{1,0:T(8,128)S(1)}, f32[128,256]{1,0:T(8,128)S(1)}, u32[]{:S(2)}, u32[]{:S(2)}) collective-permute-start(f32[128,256]{1,0:T(8,128)S(1)} %slice.33), channel_id=1, source_target_pairs={{0,2},{1,3},{2,4},{3,5},{4,6},{5,7},{6,0},{7,1},{8,10},{9,11},{10,... | collective-permute-start | bytes 393224 | tf_op jit(solution)/shard_map/ppermute | solution.py:29
  52.8 34.6 %collective-permute-start.9 = (f32[128,256]{1,0:T(8,128)S(1)}, f32[128,256]{1,0:T(8,128)S(1)}, u32[]{:S(2)}, u32[]{:S(2)}) collective-permute-start(f32[128,256]{1,0:T(8,128)S(1)} %slice.32), channel_id=1, source_target_pairs={{0,6},{1,7},{2,0},{3,1},{4,2},{5,3},{6,4},{7,5},{8,14},{9,15},{10,... | collective-permute-start | bytes 393224 | tf_op jit(solution)/shard_map/ppermute | solution.py:29
  56.0 29.4 %collective-permute-start.5 = (f32[256,256]{1,0:T(8,128)}, f32[256,256]{1,0:T(8,128)S(1)}, u32[]{:S(2)}, u32[]{:S(2)}) collective-permute-start(f32[256,256]{1,0:T(8,128)} %collective-permute-done.4), channel_id=1, source_target_pairs={{0,1},{1,2},{2,3},{3,4},{4,5},{5,6},{6,7},{7,0},{8,9},{9,10},{10,1... | collective-permute-start | bytes 786440 | tf_op jit(solution)/shard_map/ppermute | solution.py:29
  59.3 28.1 %collective-permute-start.8 = (f32[256,256]{1,0:T(8,128)}, f32[256,256]{1,0:T(8,128)S(1)}, u32[]{:S(2)}, u32[]{:S(2)}) collective-permute-start(f32[256,256]{1,0:T(8,128)} %collective-permute-done.7), channel_id=1, source_target_pairs={{0,7},{1,0},{2,1},{3,2},{4,3},{5,4},{6,5},{7,6},{8,15},{9,8},{10,9... | collective-permute-start | bytes 786440 | tf_op jit(solution)/shard_map/ppermute | solution.py:29
  91.4 5.6 %collective-permute-start.11 = (f32[768,128]{1,0:T(8,128)}, f32[768,128]{1,0:T(8,128)S(1)}, u32[]{:S(2)}, u32[]{:S(2)}) collective-permute-start(f32[768,128]{1,0:T(8,128)} %pad_maximum_fusion), channel_id=1, source_target_pairs={{0,8},{8,0},{1,9},{9,1},{2,10},{10,2},{3,11},{11,3},{4,12},{12,4},... | collective-permute-start | bytes 1179656 | tf_op jit(solution)/shard_map/ppermute | solution.py:77
  118.8 24.9 %copy-start = (f32[2,256,256]{2,1,0:T(8,128)S(1)}, f32[2,256,256]{2,1,0:T(8,128)}, u32[]{:S(2)}) copy-start(f32[2,256,256]{2,1,0:T(8,128)} %broadcast_select_fusion) | copy-start | bytes 1572868
where the time goes:
time: 147 us
  starting transfers between devices  48.9 us (33%)
  blocking collectives  46.5 us (32%)
  waiting for transfers between devices  31 us (21%)
  matrix products  9.29 us (6%)
  local copies, waits for them, and re-layouts  8.46 us (6%)
  other arithmetic  1.9 us (1%)
    all_to_all x2, blocking collectives, reduce_rows(): lax.all_to_all(pieces, PLANE, split_axis=0, concat_axis=0, tiled=True)  40.3 us
    ppermute x8, starting transfers between devices, shift(): lax.ppermute(value, 'z', [(slot, (slot + by) % count) for slot in range(c...  30.5 us
    ppermute x8, waiting for transfers between devices, shift(): lax.ppermute(value, 'z', [(slot, (slot + by) % count) for slot in range(c...  20.9 us
    ppermute x3, starting transfers between devices, scatter_quarters(): piece = lax.ppermute(pieces[step], 'z', [(0, step), (last, last - step)])  12.5 us
    ppermute x3, waiting for transfers between devices, scatter_quarters(): piece = lax.ppermute(pieces[step], 'z', [(0, step), (last, last - step)])  10.1 us
    dot_general x11, matrix products, dot(): lax.dot_general(left, right, (dims, ((), ())), precision=lax.Precision.HI...  9.29 us
    all_gather x1, blocking collectives, reduce_rows(): lax.all_gather(pieces.reshape(rows, columns), 'c', axis=1, tiled=True)  6.22 us
    all_to_all x1, starting transfers between devices, per_device(): tiles = lax.all_to_all(tiles, 'z', split_axis=0, concat_axis=0, tiled=True)  3.57 us
  transfers between devices with their start and end apart: 13, of which 3 were waited for; matrix products, arithmetic and copies ran while one was open for 8% of the time, Pallas kernels for 0%

commit v1 on v0

--- a/solution.py
+++ b/solution.py
@@ -82,7 +82,16 @@
     pieces = lax.all_to_all(pieces, PLANE, split_axis=0, concat_axis=0, tiled=True)
     pieces = jnp.broadcast_to(pieces.sum(0)[None], pieces.shape)
     pieces = lax.all_to_all(pieces, PLANE, split_axis=0, concat_axis=0, tiled=True)
-    return lax.all_gather(pieces.reshape(rows, columns), "c", axis=1, tiled=True)
+    _part_ranges = lambda base_x: jnp.concatenate(
+        jax.lax.all_to_all(
+            jnp.stack([base_x for _ in range(jax.lax.axis_size("c"))]),
+            "c",
+            split_axis=0,
+            concat_axis=0,
+        ),
+        axis=1,
+    )
+    return _part_ranges(pieces.reshape(rows, columns))
 
 
 def per_device(eigvecs, panels, tfactors, owners):

time: 147 us -> 156 us (1.061)
  local copies, waits for them, and re-layouts: 8.46 us -> 14.8 us
  blocking collectives: 46.5 us -> 48.4 us
    all_to_all x0 -> x1, blocking collectives: none -> 8.23 us  [reduce_rows(): jax.lax.all_to_all(jnp.stack([base_x for _ in range(jax.lax.axis_size('c'...]
    all_gather x1 -> x0, blocking collectives: 6.22 us -> none  [reduce_rows(): lax.all_gather(pieces.reshape(rows, columns), 'c', axis=1, tiled=True)]
    slice x0 -> x5, local copies, waits for them, and re-layouts: none -> 5.66 us  [the longest x2 2.67 us: per_device(): total[2 * width:]]
where the time goes in v1:
time: 156 us
  blocking collectives  48.4 us (31%)
  starting transfers between devices  48.2 us (31%)
  waiting for transfers between devices  31 us (20%)
  local copies, waits for them, and re-layouts  14.8 us (9%)
  matrix products  10.5 us (7%)
  other arithmetic  1.95 us (1%)
    all_to_all x2, blocking collectives, reduce_rows(): lax.all_to_all(pieces, PLANE, split_axis=0, concat_axis=0, tiled=True)  40.2 us
    ppermute x8, starting transfers between devices, shift(): lax.ppermute(value, 'z', [(slot, (slot + by) % count) for slot in range(c...  30.5 us
    ppermute x8, waiting for transfers between devices, shift(): lax.ppermute(value, 'z', [(slot, (slot + by) % count) for slot in range(c...  20.9 us
    ppermute x3, starting transfers between devices, scatter_quarters(): piece = lax.ppermute(pieces[step], 'z', [(0, step), (last, last - step)])  11.8 us
    dot_general x11, matrix products, dot(): lax.dot_general(left, right, (dims, ((), ())), precision=lax.Precision.HI...  10.5 us
    ppermute x3, waiting for transfers between devices, scatter_quarters(): piece = lax.ppermute(pieces[step], 'z', [(0, step), (last, last - step)])  10.1 us
    all_to_all x1, blocking collectives, reduce_rows(): jax.lax.all_to_all(jnp.stack([base_x for _ in range(jax.lax.axis_size('c'...  8.23 us
    all_to_all x1, starting transfers between devices, per_device(): tiles = lax.all_to_all(tiles, 'z', split_axis=0, concat_axis=0, tiled=True)  3.57 us
  transfers between devices with their start and end apart: 13, of which 3 were waited for; matrix products, arithmetic and copies ran while one was open for 8% of the time, Pallas kernels for 0%

profile of v1, /device:TPU:1, one launch (start us, length us, event | category | flops | bytes accessed | tf_op | source)
XLA Modules:
  0.0 155.5 jit_solution(17332426812511023034)
XLA Ops:
  0.0 1.4 dynamic-slice_bitcast_fusion
  1.4 8.5 %collective-permute-start = (f32[256,256]{1,0:T(8,128)S(1)}, f32[256,256]{1,0:T(8,128)S(1)}, u32[]{:S(2)}, u32[]{:S(2)}) collective-permute-start(f32[256,256]{1,0:T(8,128)S(1)} %get-tuple-element.13), channel_id=1, source_target_pairs={{0,3},{7,4},{8,11},{15,12},{16,19},{23,20},{24,27},{31,28},{32,35}... | collective-permute-start | bytes 786440 | tf_op jit(solution)/shard_map/ppermute | solution.py:44
  9.9 1.3 collective-permute-start.1
  11.2 2.0 %collective-permute-start.2 = (f32[256,256]{1,0:T(8,128)S(1)}, f32[256,256]{1,0:T(8,128)}, u32[]{:S(2)}, u32[]{:S(2)}) collective-permute-start(f32[256,256]{1,0:T(8,128)S(1)} %get-tuple-element.15), channel_id=1, source_target_pairs={{0,1},{7,6},{8,9},{15,14},{16,17},{23,22},{24,25},{31,30},{32,33},... | collective-permute-start | bytes 786440 | tf_op jit(solution)/shard_map/ppermute | solution.py:44
  13.2 0.1 iota_compare_fusion
  13.3 0.0 copy-start.6
  13.3 1.1 copy.14
  14.4 0.0 copy-done.4
  14.4 0.8 broadcast_select_fusion
  15.2 0.0 collective-permute-done
  15.2 5.2 %collective-permute-done.1 = f32[256,256]{1,0:T(8,128)S(1)} collective-permute-done((f32[256,256]{1,0:T(8,128)S(1)}, f32[256,256]{1,0:T(8,128)S(1)}, u32[]{:S(2)}, u32[]{:S(2)}) %collective-permute-start.1) | collective-permute-done | bytes 262176 | tf_op jit(solution)/shard_map/ppermute | solution.py:44
  20.4 0.7 copy-done.5
  21.1 4.9 %collective-permute-done.2 = f32[256,256]{1,0:T(8,128)} collective-permute-done((f32[256,256]{1,0:T(8,128)S(1)}, f32[256,256]{1,0:T(8,128)}, u32[]{:S(2)}, u32[]{:S(2)}) %collective-permute-start.2) | collective-permute-done | bytes 262176 | tf_op jit(solution)/shard_map/ppermute | solution.py:44
  26.0 0.1 select_select_fusion
  26.1 1.9 %collective-permute-start.4 = (f32[256,256]{1,0:T(8,128)S(1)}, f32[256,256]{1,0:T(8,128)}, u32[]{:S(2)}, u32[]{:S(2)}) collective-permute-start(f32[256,256]{1,0:T(8,128)S(1)} %select_select_fusion), channel_id=1, source_target_pairs={{0,2},{1,3},{2,4},{3,5},{4,6},{5,7},{6,0},{7,1},{8,10},{9,11},{10,... | collective-permute-start | bytes 786440 | tf_op jit(solution)/shard_map/ppermute | solution.py:29
  28.0 8.2 %collective-permute-start.7 = (f32[256,256]{1,0:T(8,128)S(1)}, f32[256,256]{1,0:T(8,128)}, u32[]{:S(2)}, u32[]{:S(2)}) collective-permute-start(f32[256,256]{1,0:T(8,128)S(1)} %select_select_fusion), channel_id=1, source_target_pairs={{0,6},{1,7},{2,0},{3,1},{4,2},{5,3},{6,4},{7,5},{8,14},{9,15},{10,... | collective-permute-start | bytes 786440 | tf_op jit(solution)/shard_map/ppermute | solution.py:29
  36.2 2.5 %collective-permute-start.3 = (f32[256,256]{1,0:T(8,128)S(1)}, f32[256,256]{1,0:T(8,128)}, u32[]{:S(2)}, u32[]{:S(2)}) collective-permute-start(f32[256,256]{1,0:T(8,128)S(1)} %select_select_fusion), channel_id=1, source_target_pairs={{0,1},{1,2},{2,3},{3,4},{4,5},{5,6},{6,7},{7,0},{8,9},{9,10},{10,1... | collective-permute-start | bytes 786440 | tf_op jit(solution)/shard_map/ppermute | solution.py:29
  38.9 4.0 %collective-permute-start.6 = (f32[256,256]{1,0:T(8,128)S(1)}, f32[256,256]{1,0:T(8,128)}, u32[]{:S(2)}, u32[]{:S(2)}) collective-permute-start(f32[256,256]{1,0:T(8,128)S(1)} %select_select_fusion), channel_id=1, source_target_pairs={{0,7},{1,0},{2,1},{3,2},{4,3},{5,4},{6,5},{7,6},{8,15},{9,8},{10,9... | collective-permute-start | bytes 786440 | tf_op jit(solution)/shard_map/ppermute | solution.py:29
  42.9 3.6 %all-to-all-start = ((f32[8,128,256]{2,1,0:T(8,128)}), f32[8,128,256]{2,1,0:T(8,128)S(1)}, u32[]{:S(2)}, u32[]{:S(2)}) async-start(f32[8,128,256]{2,1,0:T(8,128)} %bitcast.77), calls=%async_computation | async-start | bytes 2097152 | tf_op jit(solution)/shard_map/all_to_all | solution.py:105
  46.5 0.2 broadcast_in_dim.44
  46.7 0.0 collective-permute-done.4
  46.7 0.9 slice.45
  47.6 4.2 %collective-permute-start.10 = (f32[128,256]{1,0:T(8,128)S(1)}, f32[128,256]{1,0:T(8,128)S(1)}, u32[]{:S(2)}, u32[]{:S(2)}) collective-permute-start(f32[128,256]{1,0:T(8,128)S(1)} %slice.45), channel_id=1, source_target_pairs={{0,2},{1,3},{2,4},{3,5},{4,6},{5,7},{6,0},{7,1},{8,10},{9,11},{10,... | collective-permute-start | bytes 393224 | tf_op jit(solution)/shard_map/ppermute | solution.py:29
  51.8 0.0 collective-permute-done.7
  51.8 0.9 slice.44
  52.8 3.2 %collective-permute-start.9 = (f32[128,256]{1,0:T(8,128)S(1)}, f32[128,256]{1,0:T(8,128)S(1)}, u32[]{:S(2)}, u32[]{:S(2)}) collective-permute-start(f32[128,256]{1,0:T(8,128)S(1)} %slice.44), channel_id=1, source_target_pairs={{0,6},{1,7},{2,0},{3,1},{4,2},{5,3},{6,4},{7,5},{8,14},{9,15},{10,... | collective-permute-start | bytes 393224 | tf_op jit(solution)/shard_map/ppermute | solution.py:29
  56.0 3.3 %collective-permute-start.5 = (f32[256,256]{1,0:T(8,128)}, f32[256,256]{1,0:T(8,128)S(1)}, u32[]{:S(2)}, u32[]{:S(2)}) collective-permute-start(f32[256,256]{1,0:T(8,128)} %collective-permute-done.4), channel_id=1, source_target_pairs={{0,1},{1,2},{2,3},{3,4},{4,5},{5,6},{6,7},{7,0},{8,9},{9,10},{10,1... | collective-permute-start | bytes 786440 | tf_op jit(solution)/shard_map/ppermute | solution.py:29
  59.3 0.0 collective-permute-done.3
  59.3 3.2 %collective-permute-start.8 = (f32[256,256]{1,0:T(8,128)}, f32[256,256]{1,0:T(8,128)S(1)}, u32[]{:S(2)}, u32[]{:S(2)}) collective-permute-start(f32[256,256]{1,0:T(8,128)} %collective-permute-done.7), channel_id=1, source_target_pairs={{0,7},{1,0},{2,1},{3,2},{4,3},{5,4},{6,5},{7,6},{8,15},{9,8},{10,9... | collective-permute-start | bytes 786440 | tf_op jit(solution)/shard_map/ppermute | solution.py:29
  62.5 1.0 bitcast_dynamic-update-slice_fusion.5
  63.5 1.0 bitcast_dynamic-update-slice_fusion.4
  64.5 20.9 %collective-permute-done.5 = f32[256,256]{1,0:T(8,128)S(1)} collective-permute-done((f32[256,256]{1,0:T(8,128)}, f32[256,256]{1,0:T(8,128)S(1)}, u32[]{:S(2)}, u32[]{:S(2)}) %collective-permute-start.5) | collective-permute-done | bytes 262176 | tf_op jit(solution)/shard_map/ppermute | solution.py:29
  85.4 0.0 collective-permute-done.6
  85.4 1.0 bitcast_dynamic-update-slice_fusion.2
  86.4 1.0 bitcast_dynamic-update-slice_fusion.1
  87.3 0.0 collective-permute-done.8
  87.4 0.0 collective-permute-done.10
  87.4 0.0 collective-permute-done.9
  87.4 1.2 fusion.1
  88.6 0.0 all-to-all-done
  88.6 1.0 fusion.10
  89.6 1.0 fusion.3
  90.6 0.8 pad_maximum_fusion.1
  91.4 2.4 %collective-permute-start.11 = (f32[768,128]{1,0:T(8,128)}, f32[768,128]{1,0:T(8,128)S(1)}, u32[]{:S(2)}, u32[]{:S(2)}) collective-permute-start(f32[768,128]{1,0:T(8,128)} %pad_maximum_fusion.1), channel_id=1, source_target_pairs={{0,8},{8,0},{1,9},{9,1},{2,10},{10,2},{3,11},{11,3},{4,12},{12,4},... | collective-permute-start | bytes 1179656 | tf_op jit(solution)/shard_map/ppermute | solution.py:77
  93.8 1.2 fusion.5
  95.0 1.0 fusion.12
  96.0 1.0 fusion.7
  97.0 0.0 collective-permute-done.11
  97.1 21.7 %all_to_all.20 = f32[32,24,128]{2,1,0:T(8,128)S(1)} all-to-all(f32[32,24,128]{2,1,0:T(8,128)S(1)} %bitcast.93), channel_id=1, replica_groups=mesh['x'=4,'y'=8,'c'=2,'z'=8] {'x','y'}, dimensions={0} | all-to-all | bytes 786432 | tf_op jit(solution)/shard_map/all_to_all | solution.py:82
  118.9 18.5 %all_to_all.21 = f32[32,24,128]{2,1,0:T(8,128)S(1)} all-to-all(f32[32,24,128]{2,1,0:T(8,128)S(1)} %broadcast_in_dim.53), channel_id=1, replica_groups=mesh['x'=4,'y'=8,'c'=2,'z'=8] {'x','y'}, dimensions={0} | all-to-all | bytes 786432 | tf_op jit(solution)/shard_map/all_to_all | solution.py:84
  137.3 0.1 pad_maximum_fusion
  137.4 8.2 %all_to_all.22 = f32[2,768,128]{2,1,0:T(8,128)S(1)} all-to-all(f32[2,768,128]{2,1,0:T(8,128)S(1)} %pad_maximum_fusion), channel_id=1, replica_groups=mesh['x'=4,'y'=8,'c'=2,'z'=8] {'c'}, dimensions={0} | all-to-all | bytes 1572864 | tf_op jit(solution)/shard_map/all_to_all | solution.py:86
  145.6 0.9 fusion.45
  146.5 1.1 copy.9
  147.6 0.8 copy.11
  148.4 1.1 copy.8
  149.5 1.8 %copy.10 = f32[256,2,128]{0,2,1:T(8,128)} copy(f32[256,2,128]{2,0,1:T(8,128)} %get-tuple-element.25) | data formatting | bytes 524288 | tf_op jit(solution)/shard_map/slice | solution.py:113
  151.3 1.3 fusion.33
  152.6 0.0 copy-start
  152.7 0.6 convolution_subtract_fusion.1
  153.3 0.4 convolution_subtract_fusion.2
  153.7 0.0 copy-done
  153.7 0.3 fusion.31
  154.0 1.6 %convolution_subtract_fusion = f32[1024,256]{1,0:T(8,128)} fusion(f32[1024,256]{1,0:T(8,128)S(1)} %convolution_subtract_fusion.1, f32[256,256]{1,0:T(8,128)S(1)} %fusion.31, f32[2,1024,256]{2,1,0:T(8,128)S(1)} %bitcast.86, s32[]{:T(128)S(6)} %select_n.156), kind=kOutput, calls=%fused_computation | convolution fusion | flops 402915328 | bytes 3407876 | tf_op jit(solution)/shard_map/dot_general | solution.py:10
  (17 shorter events, 0.2 us)
Async XLA Ops:
  0.0 13.3 %copy-start.1 = (f32[128,2048]{1,0:T(8,128)S(1)}, f32[128,2048]{1,0:T(8,128)}, u32[]{:S(2)}) copy-start(f32[128,2048]{1,0:T(8,128)} %param.4) | copy-start | bytes 3145732
  0.0 14.4 %copy-start.4 = (f32[2,256,256]{2,1,0:T(8,128)S(1)}, f32[2,256,256]{2,1,0:T(8,128)}, u32[]{:S(2)}) copy-start(f32[2,256,256]{2,1,0:T(8,128)} %param.6) | copy-start | bytes 1572868
  1.4 13.9 %collective-permute-start = (f32[256,256]{1,0:T(8,128)S(1)}, f32[256,256]{1,0:T(8,128)S(1)}, u32[]{:S(2)}, u32[]{:S(2)}) collective-permute-start(f32[256,256]{1,0:T(8,128)S(1)} %get-tuple-element.13), channel_id=1, source_target_pairs={{0,3},{7,4},{8,11},{15,12},{16,19},{23,20},{24,27},{31,28},{32,35}... | collective-permute-start | bytes 786440 | tf_op jit(solution)/shard_map/ppermute | solution.py:44
  9.9 10.6 %collective-permute-start.1 = (f32[256,256]{1,0:T(8,128)S(1)}, f32[256,256]{1,0:T(8,128)S(1)}, u32[]{:S(2)}, u32[]{:S(2)}) collective-permute-start(f32[256,256]{1,0:T(8,128)S(1)} %get-tuple-element.14), channel_id=1, source_target_pairs={{0,2},{7,5},{8,10},{15,13},{16,18},{23,21},{24,26},{31,29},{32,34}... | collective-permute-start | bytes 786440 | tf_op jit(solution)/shard_map/ppermute | solution.py:44
  11.2 14.9 %collective-permute-start.2 = (f32[256,256]{1,0:T(8,128)S(1)}, f32[256,256]{1,0:T(8,128)}, u32[]{:S(2)}, u32[]{:S(2)}) collective-permute-start(f32[256,256]{1,0:T(8,128)S(1)} %get-tuple-element.15), channel_id=1, source_target_pairs={{0,1},{7,6},{8,9},{15,14},{16,17},{23,22},{24,25},{31,30},{32,33},... | collective-permute-start | bytes 786440 | tf_op jit(solution)/shard_map/ppermute | solution.py:44
  13.3 25.5 %copy-start.6 = (s32[2]{0:T(128)S(1)}, s32[2]{0:T(128)}, u32[]{:S(2)}) copy-start(s32[2]{0:T(128)} %param.7) | copy-start | bytes 28
  20.4 0.7 copy-start.5
  26.1 20.6 %collective-permute-start.4 = (f32[256,256]{1,0:T(8,128)S(1)}, f32[256,256]{1,0:T(8,128)}, u32[]{:S(2)}, u32[]{:S(2)}) collective-permute-start(f32[256,256]{1,0:T(8,128)S(1)} %select_select_fusion), channel_id=1, source_target_pairs={{0,2},{1,3},{2,4},{3,5},{4,6},{5,7},{6,0},{7,1},{8,10},{9,11},{10,... | collective-permute-start | bytes 786440 | tf_op jit(solution)/shard_map/ppermute | solution.py:29
  28.0 23.8 %collective-permute-start.7 = (f32[256,256]{1,0:T(8,128)S(1)}, f32[256,256]{1,0:T(8,128)}, u32[]{:S(2)}, u32[]{:S(2)}) collective-permute-start(f32[256,256]{1,0:T(8,128)S(1)} %select_select_fusion), channel_id=1, source_target_pairs={{0,6},{1,7},{2,0},{3,1},{4,2},{5,3},{6,4},{7,5},{8,14},{9,15},{10,... | collective-permute-start | bytes 786440 | tf_op jit(solution)/shard_map/ppermute | solution.py:29
  36.2 23.0 %collective-permute-start.3 = (f32[256,256]{1,0:T(8,128)S(1)}, f32[256,256]{1,0:T(8,128)}, u32[]{:S(2)}, u32[]{:S(2)}) collective-permute-start(f32[256,256]{1,0:T(8,128)S(1)} %select_select_fusion), channel_id=1, source_target_pairs={{0,1},{1,2},{2,3},{3,4},{4,5},{5,6},{6,7},{7,0},{8,9},{9,10},{10,1... | collective-permute-start | bytes 786440 | tf_op jit(solution)/shard_map/ppermute | solution.py:29
  38.9 46.5 %collective-permute-start.6 = (f32[256,256]{1,0:T(8,128)S(1)}, f32[256,256]{1,0:T(8,128)}, u32[]{:S(2)}, u32[]{:S(2)}) collective-permute-start(f32[256,256]{1,0:T(8,128)S(1)} %select_select_fusion), channel_id=1, source_target_pairs={{0,7},{1,0},{2,1},{3,2},{4,3},{5,4},{6,5},{7,6},{8,15},{9,8},{10,9... | collective-permute-start | bytes 786440 | tf_op jit(solution)/shard_map/ppermute | solution.py:29
  42.9 45.7 %all-to-all-start = ((f32[8,128,256]{2,1,0:T(8,128)}), f32[8,128,256]{2,1,0:T(8,128)S(1)}, u32[]{:S(2)}, u32[]{:S(2)}) async-start(f32[8,128,256]{2,1,0:T(8,128)} %bitcast.77), calls=%async_computation | async-start | bytes 2097152 | tf_op jit(solution)/shard_map/all_to_all | solution.py:105
  47.6 39.7 %collective-permute-start.10 = (f32[128,256]{1,0:T(8,128)S(1)}, f32[128,256]{1,0:T(8,128)S(1)}, u32[]{:S(2)}, u32[]{:S(2)}) collective-permute-start(f32[128,256]{1,0:T(8,128)S(1)} %slice.45), channel_id=1, source_target_pairs={{0,2},{1,3},{2,4},{3,5},{4,6},{5,7},{6,0},{7,1},{8,10},{9,11},{10,... | collective-permute-start | bytes 393224 | tf_op jit(solution)/shard_map/ppermute | solution.py:29
  52.8 34.6 %collective-permute-start.9 = (f32[128,256]{1,0:T(8,128)S(1)}, f32[128,256]{1,0:T(8,128)S(1)}, u32[]{:S(2)}, u32[]{:S(2)}) collective-permute-start(f32[128,256]{1,0:T(8,128)S(1)} %slice.44), channel_id=1, source_target_pairs={{0,6},{1,7},{2,0},{3,1},{4,2},{5,3},{6,4},{7,5},{8,14},{9,15},{10,... | collective-permute-start | bytes 393224 | tf_op jit(solution)/shard_map/ppermute | solution.py:29
  56.0 29.4 %collective-permute-start.5 = (f32[256,256]{1,0:T(8,128)}, f32[256,256]{1,0:T(8,128)S(1)}, u32[]{:S(2)}, u32[]{:S(2)}) collective-permute-start(f32[256,256]{1,0:T(8,128)} %collective-permute-done.4), channel_id=1, source_target_pairs={{0,1},{1,2},{2,3},{3,4},{4,5},{5,6},{6,7},{7,0},{8,9},{9,10},{10,1... | collective-permute-start | bytes 786440 | tf_op jit(solution)/shard_map/ppermute | solution.py:29
  59.3 28.1 %collective-permute-start.8 = (f32[256,256]{1,0:T(8,128)}, f32[256,256]{1,0:T(8,128)S(1)}, u32[]{:S(2)}, u32[]{:S(2)}) collective-permute-start(f32[256,256]{1,0:T(8,128)} %collective-permute-done.7), channel_id=1, source_target_pairs={{0,7},{1,0},{2,1},{3,2},{4,3},{5,4},{6,5},{7,6},{8,15},{9,8},{10,9... | collective-permute-start | bytes 786440 | tf_op jit(solution)/shard_map/ppermute | solution.py:29
  91.4 5.6 %collective-permute-start.11 = (f32[768,128]{1,0:T(8,128)}, f32[768,128]{1,0:T(8,128)S(1)}, u32[]{:S(2)}, u32[]{:S(2)}) collective-permute-start(f32[768,128]{1,0:T(8,128)} %pad_maximum_fusion.1), channel_id=1, source_target_pairs={{0,8},{8,0},{1,9},{9,1},{2,10},{10,2},{3,11},{11,3},{4,12},{12,4},... | collective-permute-start | bytes 1179656 | tf_op jit(solution)/shard_map/ppermute | solution.py:77
  151.3 2.0 %copy-start.2 = (f32[256,256]{1,0:T(8,128)S(1)}, f32[256,256]{1,0:T(8,128)}, u32[]{:S(2)}) copy-start(f32[256,256]{1,0:T(8,128)} %copy.11) | copy-start | bytes 786436
  151.3 2.0 %copy-start.3 = (f32[256,2,128]{0,2,1:T(8,128)S(1)}, f32[256,2,128]{0,2,1:T(8,128)}, u32[]{:S(2)}) copy-start(f32[256,2,128]{0,2,1:T(8,128)} %copy.10) | copy-start | bytes 786436
  152.6 1.0 copy-start
